TPU v7x, 256 devices: a whole 4x4x8 slice. The times are simulated.
256 devices in a mesh: tm: 16 (over x_hi, z), inner: 16 (over y, x_lo, core).
Axes of the slice: x: 4 (x_hi: 2, x_lo: 2; x = x_hi * 2 + x_lo), y: 4, z: 8, core: 2. Of those that a mesh axis runs over, the one named last changes fastest.
Arguments:
- start_panels: float32 [16, 192, 2048], P('tm', None, 'inner'), may hold values from -6 to 6
- kinetic: float32 [2048, 2048], P('inner')
- fields: int32 [16, 2048], P('tm'), may hold values from -1 to 1, as said below
Outputs:
- orbitals: float32 [16, 8, 192, 2048], P('tm', None, None, 'inner')
- log_scales: float32 [16, 8, 192], P('tm')
Inputs may be any that keep to these rules, and one draw needn't show every extreme that they name: `fields`: each entry is -1 or +1.
All inputs are finite; a program needn't handle non-finite values.
Results may differ from a plain program's by a relative error of at most 0.0003.
Values sent between devices are 32-bit elements; how exact they have to be, the bound alone decides.
No kernel may reach another device: no remote copies, remote signals or barrier semaphores. Data moves between devices by JAX's collectives and lax.ppermute only.
A program may use at most 128 MiB of HBM per device.

v0:
```python
import math
import jax
import jax.numpy as jnp
from jax import lax
from jax.sharding import PartitionSpec as P

coupling = 0.17725


def from_behind(block, axis, distance):
    devices = range(lax.axis_size(axis))
    route = [((i - distance) % len(devices), i) for i in devices]
    return lax.ppermute(block, axis, route)


def contract_last(left, right):
    return lax.dot_general(
        left,
        right,
        (((1,), (1,)), ((), ())),
        precision=lax.Precision.HIGHEST,
        preferred_element_type=jnp.float32,
    )


def factor_panel(panel, gram_matrix):
    lower = jnp.linalg.cholesky(gram_matrix)
    orthonormal = lax.linalg.triangular_solve(lower, panel, left_side=True, lower=True)
    return (orthonormal, jnp.log(jnp.diagonal(lower)))


def on_device(start_panels, kinetic, fields):
    rows = kinetic.shape[0]
    sites = kinetic.shape[1]
    rank = lax.axis_index("inner")
    hops = lax.axis_size("tm") // 2
    first = rank * rows
    scales = jnp.exp(coupling * fields.astype(jnp.float32))
    orbit_list = []
    log_list = []
    own_scales = lax.dynamic_slice_in_dim(scales, first, rows, 1)
    own_block = start_panels[0]
    for hop in range(hops):
        own_block = (
            contract_last(lax.all_gather(own_block, "inner", axis=1, tiled=True), kinetic)
            * own_scales[0][None, :]
        )
        gram_matrix = lax.psum(contract_last(own_block, own_block), "inner")
        own_block, log_diag = factor_panel(own_block, gram_matrix)
        orbit_list.append(math.sqrt(sites) * own_block)
        log_list.append(log_diag)
        if hop + 1 < hops:
            own_block = from_behind(own_block, "tm", 1)
    return (jnp.stack(orbit_list, 0)[None], jnp.stack(log_list, 0)[None])


def solution(mesh):
    placed = (P("tm", None, "inner"), P("inner", None), P("tm", None))
    return jax.shard_map(
        on_device,
        mesh=mesh,
        in_specs=placed,
        out_specs=(P("tm", None, None, "inner"), P("tm", None, None)),
        check_vma=False,
    )
```

profile of v0, /device:TPU:1, one launch (start us, length us, event | category | flops | bytes accessed | tf_op | source)
XLA Modules:
  0.0 1765.3 jit_solution(9818129227126943744)
XLA Ops:
  8.6 43.4 %all-gather.24.cloned.1.call-done = f32[1,192,2048]{2,1,0:T(8,128)} async-done(((f32[1,192,128]{2,1,0:T(8,128)}), f32[1,192,2048]{2,1,0:T(8,128)}) %all-gather.24.cloned.1.call-update) | async-done | bytes 1572880 | tf_op jit(solution)/shard_map/all_gather | solution.py:45
  52.0 2.8 fusion.2
  56.0 115.6 %all-reduce.12.cloned.1.call-done = f32[192,192]{0,1:T(8,128)} async-done(((f32[192,192]{0,1:T(8,128)}), f32[192,192]{0,1:T(8,128)}) %all-reduce.12.cloned.1.call-update) | async-done | bytes 147472 | tf_op jit(solution)/shard_map/psum | solution.py:48
  173.6 11.7 cholesky.412
  185.9 9.8 custom-call.41
  196.2 5.8 cholesky.432
  204.1 19.7 %custom-call.42 = f32[2,128,128]{1,2,0:T(8,128)S(1)} custom-call(f32[2,128,128]{2,1,0:T(8,128)S(1)} %pad_maximum_fusion), custom_call_target="InvertDiagBlocksLowerTriangular" | custom-call | tf_op jit(solution)/shard_map/triangular_solve/custom-call.0 | solution.py:28
  225.7 6.2 collective-permute-done
  232.8 36.1 %all-gather.10.cloned.1.call-done = f32[192,2048]{1,0:T(8,128)} async-done(((f32[192,128]{1,0:T(8,128)}), f32[192,2048]{1,0:T(8,128)}) %all-gather.10.cloned.1.call-update) | async-done | bytes 1572880 | tf_op jit(solution)/shard_map/all_gather | solution.py:45
  268.9 2.8 convolution_multiply_fusion.6
  272.8 115.6 %all-reduce.14.cloned.1.call-done = f32[192,192]{0,1:T(8,128)} async-done(((f32[192,192]{0,1:T(8,128)}), f32[192,192]{0,1:T(8,128)}) %all-reduce.14.cloned.1.call-update) | async-done | bytes 147472 | tf_op jit(solution)/shard_map/psum | solution.py:48
  390.5 11.7 cholesky.450
  402.9 9.8 custom-call.43
  413.1 5.8 cholesky.470
  421.0 19.7 %custom-call.44 = f32[2,128,128]{1,2,0:T(8,128)S(1)} custom-call(f32[2,128,128]{2,1,0:T(8,128)S(1)} %pad_maximum_fusion.1), custom_call_target="InvertDiagBlocksLowerTriangular" | custom-call | tf_op jit(solution)/shard_map/triangular_solve/custom-call.0 | solution.py:28
  441.5 10.5 collective-permute-start.1
  452.0 6.2 collective-permute-done.1
  458.9 36.4 %all-gather.12.cloned.1.call-done = f32[192,2048]{1,0:T(8,128)} async-done(((f32[192,128]{1,0:T(8,128)}), f32[192,2048]{1,0:T(8,128)}) %all-gather.12.cloned.1.call-update) | async-done | bytes 1572880 | tf_op jit(solution)/shard_map/all_gather | solution.py:45
  495.3 2.8 convolution_multiply_fusion.5
  499.2 115.4 %all-reduce.16.cloned.1.call-done = f32[192,192]{0,1:T(8,128)} async-done(((f32[192,192]{0,1:T(8,128)}), f32[192,192]{0,1:T(8,128)}) %all-reduce.16.cloned.1.call-update) | async-done | bytes 147472 | tf_op jit(solution)/shard_map/psum | solution.py:48
  616.6 11.7 cholesky.488
  629.0 9.8 custom-call.45
  639.2 5.8 cholesky.508
  647.2 19.7 %custom-call.46 = f32[2,128,128]{1,2,0:T(8,128)S(1)} custom-call(f32[2,128,128]{2,1,0:T(8,128)S(1)} %pad_maximum_fusion.2), custom_call_target="InvertDiagBlocksLowerTriangular" | custom-call | tf_op jit(solution)/shard_map/triangular_solve/custom-call.0 | solution.py:28
  668.7 6.2 collective-permute-done.2
  676.0 36.0 %all-gather.14.cloned.1.call-done = f32[192,2048]{1,0:T(8,128)} async-done(((f32[192,128]{1,0:T(8,128)}), f32[192,2048]{1,0:T(8,128)}) %all-gather.14.cloned.1.call-update) | async-done | bytes 1572880 | tf_op jit(solution)/shard_map/all_gather | solution.py:45
  712.0 2.8 convolution_multiply_fusion.4
  715.9 115.6 %all-reduce.18.cloned.1.call-done = f32[192,192]{0,1:T(8,128)} async-done(((f32[192,192]{0,1:T(8,128)}), f32[192,192]{0,1:T(8,128)}) %all-reduce.18.cloned.1.call-update) | async-done | bytes 147472 | tf_op jit(solution)/shard_map/psum | solution.py:48
  833.5 11.7 cholesky.526
  845.9 9.8 custom-call.47
  856.1 5.8 cholesky.546
  864.1 19.7 %custom-call.48 = f32[2,128,128]{1,2,0:T(8,128)S(1)} custom-call(f32[2,128,128]{2,1,0:T(8,128)S(1)} %pad_maximum_fusion.3), custom_call_target="InvertDiagBlocksLowerTriangular" | custom-call | tf_op jit(solution)/shard_map/triangular_solve/custom-call.0 | solution.py:28
  885.8 6.2 collective-permute-done.3
  892.7 36.4 %all-gather.16.cloned.1.call-done = f32[192,2048]{1,0:T(8,128)} async-done(((f32[192,128]{1,0:T(8,128)}), f32[192,2048]{1,0:T(8,128)}) %all-gather.16.cloned.1.call-update) | async-done | bytes 1572880 | tf_op jit(solution)/shard_map/all_gather | solution.py:45
  929.1 2.8 convolution_multiply_fusion.3
  932.9 115.4 %all-reduce.20.cloned.1.call-done = f32[192,192]{0,1:T(8,128)} async-done(((f32[192,192]{0,1:T(8,128)}), f32[192,192]{0,1:T(8,128)}) %all-reduce.20.cloned.1.call-update) | async-done | bytes 147472 | tf_op jit(solution)/shard_map/psum | solution.py:48
  1050.4 11.7 cholesky.564
  1062.8 9.8 custom-call.49
  1073.0 5.8 cholesky.584
  1081.0 19.7 %custom-call.50 = f32[2,128,128]{1,2,0:T(8,128)S(1)} custom-call(f32[2,128,128]{2,1,0:T(8,128)S(1)} %pad_maximum_fusion.4), custom_call_target="InvertDiagBlocksLowerTriangular" | custom-call | tf_op jit(solution)/shard_map/triangular_solve/custom-call.0 | solution.py:28
  1102.5 6.2 collective-permute-done.4
  1109.8 36.0 %all-gather.18.cloned.1.call-done = f32[192,2048]{1,0:T(8,128)} async-done(((f32[192,128]{1,0:T(8,128)}), f32[192,2048]{1,0:T(8,128)}) %all-gather.18.cloned.1.call-update) | async-done | bytes 1572880 | tf_op jit(solution)/shard_map/all_gather | solution.py:45
  1145.8 2.8 convolution_multiply_fusion.2
  1149.7 115.6 %all-reduce.22.cloned.1.call-done = f32[192,192]{0,1:T(8,128)} async-done(((f32[192,192]{0,1:T(8,128)}), f32[192,192]{0,1:T(8,128)}) %all-reduce.22.cloned.1.call-update) | async-done | bytes 147472 | tf_op jit(solution)/shard_map/psum | solution.py:48
  1267.3 11.7 cholesky.602
  1279.7 9.8 custom-call.51
  1289.9 5.8 cholesky.622
  1297.9 19.7 %custom-call.52 = f32[2,128,128]{1,2,0:T(8,128)S(1)} custom-call(f32[2,128,128]{2,1,0:T(8,128)S(1)} %pad_maximum_fusion.5), custom_call_target="InvertDiagBlocksLowerTriangular" | custom-call | tf_op jit(solution)/shard_map/triangular_solve/custom-call.0 | solution.py:28
  1319.6 6.2 collective-permute-done.5
  1326.5 36.4 %all-gather.20.cloned.1.call-done = f32[192,2048]{1,0:T(8,128)} async-done(((f32[192,128]{1,0:T(8,128)}), f32[192,2048]{1,0:T(8,128)}) %all-gather.20.cloned.1.call-update) | async-done | bytes 1572880 | tf_op jit(solution)/shard_map/all_gather | solution.py:45
  1362.8 2.8 convolution_multiply_fusion.1
  1366.7 115.6 %all-reduce.24.cloned.1.call-done = f32[192,192]{0,1:T(8,128)} async-done(((f32[192,192]{0,1:T(8,128)}), f32[192,192]{0,1:T(8,128)}) %all-reduce.24.cloned.1.call-update) | async-done | bytes 147472 | tf_op jit(solution)/shard_map/psum | solution.py:48
  1484.3 11.7 cholesky.640
  1496.8 9.8 custom-call.53
  1506.9 5.8 cholesky.660
  1515.6 20.5 %custom-call.54 = f32[2,128,128]{1,2,0:T(8,128)S(1)} custom-call(f32[2,128,128]{2,1,0:T(8,128)} %pad_maximum_fusion.6), custom_call_target="InvertDiagBlocksLowerTriangular" | custom-call | tf_op jit(solution)/shard_map/triangular_solve/custom-call.0 | solution.py:28
  1539.3 6.2 collective-permute-done.6
  1559.3 23.3 %all-gather.22.cloned.1.call-done = f32[192,2048]{1,0:T(8,128)} async-done(((f32[192,128]{1,0:T(8,128)}), f32[192,2048]{1,0:T(8,128)}) %all-gather.22.cloned.1.call-update) | async-done | bytes 1572880 | tf_op jit(solution)/shard_map/all_gather | solution.py:45
  1582.6 2.8 convolution_multiply_fusion
  1591.6 110.5 %all-reduce.26.cloned.1.call-done = f32[192,192]{0,1:T(8,128)} async-done(((f32[192,192]{0,1:T(8,128)}), f32[192,192]{0,1:T(8,128)}) %all-reduce.26.cloned.1.call-update) | async-done | bytes 147472 | tf_op jit(solution)/shard_map/psum | solution.py:48
  1704.1 11.7 cholesky.678
  1716.5 9.8 custom-call.55
  1726.7 5.8 cholesky.698
  1736.7 19.7 %custom-call.56 = f32[2,128,128]{1,2,0:T(8,128)S(1)} custom-call(f32[2,128,128]{2,1,0:T(8,128)S(1)} %pad_maximum_fusion.7), custom_call_target="InvertDiagBlocksLowerTriangular" | custom-call | tf_op jit(solution)/shard_map/triangular_solve/custom-call.0 | solution.py:28
  (247 shorter events, 82.9 us)
Async XLA Ops:
  7.2 44.9 %copy-start = (f32[128,2048]{1,0:T(8,128)S(1)}, f32[128,2048]{1,0:T(8,128)}, u32[]{:S(2)}) copy-start(f32[128,2048]{1,0:T(8,128)} %param.7) | copy-start | bytes 3145732
  7.2 44.9 %all-gather.24.cloned.1.call-start = ((), (), s32[]{:S(2)}) async-start(), calls=%async_computation.15 | async-start | bytes 1671168 | tf_op jit(solution)/shard_map/all_gather | solution.py:45
  7.9 163.6 %all-reduce.12.cloned.1.call-start = ((), (), s32[]{:S(2)}) async-start(), calls=%async_computation | async-start | bytes 393216 | tf_op jit(solution)/shard_map/psum | solution.py:48
  55.9 213.1 %all-gather.10.cloned.1.call-start = ((), (), s32[]{:S(2)}) async-start(), calls=%async_computation.1 | async-start | bytes 1671168 | tf_op jit(solution)/shard_map/all_gather | solution.py:45
  224.6 7.3 collective-permute-start
  231.8 0.6 copy-start.4
  232.5 155.9 %all-reduce.14.cloned.1.call-start = ((), (), s32[]{:S(2)}) async-start(), calls=%async_computation.2 | async-start | bytes 393216 | tf_op jit(solution)/shard_map/psum | solution.py:48
  272.8 222.5 %all-gather.12.cloned.1.call-start = ((), (), s32[]{:S(2)}) async-start(), calls=%async_computation.3 | async-start | bytes 1671168 | tf_op jit(solution)/shard_map/all_gather | solution.py:45
  441.5 16.7 collective-permute-start.1
  458.2 0.6 copy-start.5
  458.8 155.7 %all-reduce.16.cloned.1.call-start = ((), (), s32[]{:S(2)}) async-start(), calls=%async_computation.4 | async-start | bytes 393216 | tf_op jit(solution)/shard_map/psum | solution.py:48
  499.1 212.9 %all-gather.14.cloned.1.call-start = ((), (), s32[]{:S(2)}) async-start(), calls=%async_computation.5 | async-start | bytes 1671168 | tf_op jit(solution)/shard_map/all_gather | solution.py:45
  667.6 7.3 collective-permute-start.2
  674.9 0.6 copy-start.6
  675.6 155.9 %all-reduce.18.cloned.1.call-start = ((), (), s32[]{:S(2)}) async-start(), calls=%async_computation.6 | async-start | bytes 393216 | tf_op jit(solution)/shard_map/psum | solution.py:48
  715.8 213.2 %all-gather.16.cloned.1.call-start = ((), (), s32[]{:S(2)}) async-start(), calls=%async_computation.7 | async-start | bytes 1671168 | tf_op jit(solution)/shard_map/all_gather | solution.py:45
  884.5 7.4 collective-permute-start.3
  892.0 0.6 copy-start.7
  892.6 155.7 %all-reduce.20.cloned.1.call-start = ((), (), s32[]{:S(2)}) async-start(), calls=%async_computation.8 | async-start | bytes 393216 | tf_op jit(solution)/shard_map/psum | solution.py:48
  932.9 212.9 %all-gather.18.cloned.1.call-start = ((), (), s32[]{:S(2)}) async-start(), calls=%async_computation.9 | async-start | bytes 1671168 | tf_op jit(solution)/shard_map/all_gather | solution.py:45
  1101.4 7.3 collective-permute-start.4
  1108.7 0.6 copy-start.8
  1109.3 155.9 %all-reduce.22.cloned.1.call-start = ((), (), s32[]{:S(2)}) async-start(), calls=%async_computation.10 | async-start | bytes 393216 | tf_op jit(solution)/shard_map/psum | solution.py:48
  1149.6 213.2 %all-gather.20.cloned.1.call-start = ((), (), s32[]{:S(2)}) async-start(), calls=%async_computation.11 | async-start | bytes 1671168 | tf_op jit(solution)/shard_map/all_gather | solution.py:45
  1318.3 48.4 %copy-start.1 = (f32[64,128]{1,0:T(8,128)}, f32[64,128]{1,0:T(8,128)S(1)}, u32[]{:S(2)}) copy-start(f32[64,128]{1,0:T(8,128)S(1)} %fusion.74) | copy-start | bytes 98308
  1318.3 7.4 collective-permute-start.5
  1325.7 0.6 copy-start.9
  1326.4 155.9 %all-reduce.24.cloned.1.call-start = ((), (), s32[]{:S(2)}) async-start(), calls=%async_computation.12 | async-start | bytes 393216 | tf_op jit(solution)/shard_map/psum | solution.py:48
  1366.7 215.9 %all-gather.22.cloned.1.call-start = ((), (), s32[]{:S(2)}) async-start(), calls=%async_computation.13 | async-start | bytes 1671168 | tf_op jit(solution)/shard_map/all_gather | solution.py:45
  1536.1 0.7 copy-start.10
  1538.2 7.3 collective-permute-start.6
  1545.5 0.6 copy-start.3
  1546.2 155.9 %all-reduce.26.cloned.1.call-start = ((), (), s32[]{:S(2)}) async-start(), calls=%async_computation.14 | async-start | bytes 393216 | tf_op jit(solution)/shard_map/psum | solution.py:48
  1559.3 27.1 %copy-start.2 = (f32[64,128]{1,0:T(8,128)S(1)}, f32[64,128]{1,0:T(8,128)}, u32[]{:S(2)}) copy-start(f32[64,128]{1,0:T(8,128)} %copy-done.1) | copy-start | bytes 98308
Sparse Core Ops, SparseCore 0:
  9.8 42.2 all-gather.23
  56.0 115.4 all-reduce.11
  232.6 36.2 all-gather.9
  272.9 115.4 all-reduce.13
  459.0 36.2 all-gather.11
  499.2 115.3 all-reduce.15
  675.7 36.2 all-gather.13
  716.0 115.4 all-reduce.17
  892.7 36.2 all-gather.15
  933.0 115.3 all-reduce.19
  1109.5 36.2 all-gather.17
  1149.7 115.4 all-reduce.21
  1326.5 36.2 all-gather.19
  1366.8 115.4 all-reduce.23
  1546.3 36.2 all-gather.21
  1586.6 115.4 all-reduce.25
where the time goes:
time: 1780 us; the launch traced here: 1770 us
  waiting for transfers between devices  1250 us (70%)
  other arithmetic  403 us (23%)
  matrix products  39.9 us (2%)
  local copies, waits for them, and re-layouts  29.6 us (2%)
  between operations  26.1 us (1%)
  starting transfers between devices  19.3 us (1%)
    psum x8, waiting for transfers between devices, on_device(): gram_matrix = lax.psum(contract_last(own_block, own_block), 'inner')  919 us
    all_gather x8, waiting for transfers between devices, on_device(): lax.all_gather(own_block, 'inner', axis=1, tiled=True)  284 us
    another operation x56, other arithmetic, factor_panel(): lower = jnp.linalg.cholesky(gram_matrix)  230 us
    another operation x41, other arithmetic, factor_panel(): lax.linalg.triangular_solve(lower, panel, left_side=True, lower=True)  160 us
    ppermute x7, waiting for transfers between devices, from_behind(): return lax.ppermute(block, axis, route)  43.3 us
  transfers between devices with their start and end apart: 23, of which 23 were waited for; matrix products, arithmetic and copies ran while one was open for 1% of the time, Pallas kernels for 0%

commit v1 on v0

--- a/solution.py
+++ b/solution.py
@@ -45,7 +45,7 @@
             contract_last(lax.all_gather(own_block, "inner", axis=1, tiled=True), kinetic)
             * own_scales[0][None, :]
         )
-        gram_matrix = lax.psum(contract_last(own_block, own_block), "inner")
+        gram_matrix = jnp.sum(lax.all_gather(contract_last(own_block, own_block), "inner"), axis=0)
         own_block, log_diag = factor_panel(own_block, gram_matrix)
         orbit_list.append(math.sqrt(sites) * own_block)
         log_list.append(log_diag)

time: 1780 us -> 1160 us (0.65)
  waiting for transfers between devices: 1250 us -> 637 us
    psum x8 -> x0, waiting for transfers between devices: 919 us -> none  [on_device(): gram_matrix = lax.psum(contract_last(own_block, own_block), 'inner')]
    all_gather x0 -> x8, waiting for transfers between devices: none -> 292 us  [on_device(): lax.all_gather(contract_last(own_block, own_block), 'inner')]
  transfers between devices with their start and end apart: 23 -> 23, of which waited for: 23 -> 23; matrix products, arithmetic and copies ran while one was open for 1% -> 2% of each run, Pallas kernels for 0% -> 0%
where the time goes in v1:
time: 1160 us; the launch traced here: 1150 us
  waiting for transfers between devices  637 us (55%)
  other arithmetic  413 us (36%)
  matrix products  39.9 us (3%)
  between operations  26.2 us (2%)
  local copies, waits for them, and re-layouts  22.4 us (2%)
    all_gather x8, waiting for transfers between devices, on_device(): lax.all_gather(own_block, 'inner', axis=1, tiled=True)  299 us
    all_gather x8, waiting for transfers between devices, on_device(): lax.all_gather(contract_last(own_block, own_block), 'inner')  292 us
    another operation x56, other arithmetic, factor_panel(): lower = jnp.linalg.cholesky(gram_matrix)  230 us
    another operation x41, other arithmetic, factor_panel(): lax.linalg.triangular_solve(lower, panel, left_side=True, lower=True)  160 us
    ppermute x7, waiting for transfers between devices, from_behind(): return lax.ppermute(block, axis, route)  45.8 us
    dot_general x16, matrix products, contract_last(): lax.dot_general(left, right, (((1,), (1,)), ((), ())), precision=lax.Prec...  30.6 us
  transfers between devices with their start and end apart: 23, of which 23 were waited for; matrix products, arithmetic and copies ran while one was open for 2% of the time, Pallas kernels for 0%

profile of v1, /device:TPU:1, one launch (start us, length us, event | category | flops | bytes accessed | tf_op | source)
XLA Modules:
  0.0 1149.7 jit_solution(12653272847407795717)
XLA Ops:
  8.6 43.4 %all-gather.40.cloned.1.call-done = f32[1,192,2048]{2,1,0:T(8,128)} async-done(((f32[1,192,128]{2,1,0:T(8,128)}), f32[1,192,2048]{2,1,0:T(8,128)}) %all-gather.40.cloned.1.call-update) | async-done | bytes 1572880 | tf_op jit(solution)/shard_map/all_gather | solution.py:45
  52.0 2.8 fusion.2
  56.0 38.9 %all-gather.42.cloned.1.call-done = f32[3072,192]{1,0:T(8,128)} async-done(((f32[192,192]{1,0:T(8,128)}), f32[3072,192]{1,0:T(8,128)}) %all-gather.42.cloned.1.call-update) | async-done | bytes 2359312 | tf_op jit(solution)/shard_map/all_gather | solution.py:48
  97.2 11.7 %cholesky.412 = f32[128,128]{1,0:T(8,128)S(1)} custom-call(f32[128,128]{1,0:T(8,128)S(1)} %cholesky.712), custom_call_target="Cholesky" | custom-call | tf_op jit(solution)/shard_map/jit(cholesky)/cholesky | solution.py:27
  109.6 9.8 custom-call.41
  119.8 5.8 cholesky.432
  127.7 19.7 %custom-call.42 = f32[2,128,128]{1,2,0:T(8,128)S(1)} custom-call(f32[2,128,128]{2,1,0:T(8,128)S(1)} %pad_maximum_fusion), custom_call_target="InvertDiagBlocksLowerTriangular" | custom-call | tf_op jit(solution)/shard_map/triangular_solve/custom-call.0 | solution.py:28
  149.4 6.5 collective-permute-done
  157.0 36.2 %all-gather.26.cloned.1.call-done = f32[192,2048]{1,0:T(8,128)} async-done(((f32[192,128]{1,0:T(8,128)}), f32[192,2048]{1,0:T(8,128)}) %all-gather.26.cloned.1.call-update) | async-done | bytes 1572880 | tf_op jit(solution)/shard_map/all_gather | solution.py:45
  193.2 2.8 convolution_multiply_fusion.6
  197.1 38.9 %all-gather.44.cloned.1.call-done = f32[3072,192]{1,0:T(8,128)} async-done(((f32[192,192]{1,0:T(8,128)}), f32[3072,192]{1,0:T(8,128)}) %all-gather.44.cloned.1.call-update) | async-done | bytes 2359312 | tf_op jit(solution)/shard_map/all_gather | solution.py:48
  238.3 11.7 %cholesky.450 = f32[128,128]{1,0:T(8,128)S(1)} custom-call(f32[128,128]{1,0:T(8,128)S(1)} %cholesky.715), custom_call_target="Cholesky" | custom-call | tf_op jit(solution)/shard_map/jit(cholesky)/cholesky | solution.py:27
  250.7 9.8 custom-call.43
  260.9 5.8 cholesky.470
  268.9 19.7 %custom-call.44 = f32[2,128,128]{1,2,0:T(8,128)S(1)} custom-call(f32[2,128,128]{2,1,0:T(8,128)S(1)} %pad_maximum_fusion.1), custom_call_target="InvertDiagBlocksLowerTriangular" | custom-call | tf_op jit(solution)/shard_map/triangular_solve/custom-call.0 | solution.py:28
  290.6 6.5 collective-permute-done.1
  297.8 36.5 %all-gather.28.cloned.1.call-done = f32[192,2048]{1,0:T(8,128)} async-done(((f32[192,128]{1,0:T(8,128)}), f32[192,2048]{1,0:T(8,128)}) %all-gather.28.cloned.1.call-update) | async-done | bytes 1572880 | tf_op jit(solution)/shard_map/all_gather | solution.py:45
  334.3 2.8 convolution_multiply_fusion.5
  338.4 38.8 %all-gather.46.cloned.1.call-done = f32[3072,192]{1,0:T(8,128)} async-done(((f32[192,192]{1,0:T(8,128)}), f32[3072,192]{1,0:T(8,128)}) %all-gather.46.cloned.1.call-update) | async-done | bytes 2359312 | tf_op jit(solution)/shard_map/all_gather | solution.py:48
  379.5 11.7 %cholesky.488 = f32[128,128]{1,0:T(8,128)S(1)} custom-call(f32[128,128]{1,0:T(8,128)S(1)} %cholesky.718), custom_call_target="Cholesky" | custom-call | tf_op jit(solution)/shard_map/jit(cholesky)/cholesky | solution.py:27
  391.9 9.8 custom-call.45
  402.1 5.8 cholesky.508
  410.1 19.7 %custom-call.46 = f32[2,128,128]{1,2,0:T(8,128)S(1)} custom-call(f32[2,128,128]{2,1,0:T(8,128)S(1)} %pad_maximum_fusion.2), custom_call_target="InvertDiagBlocksLowerTriangular" | custom-call | tf_op jit(solution)/shard_map/triangular_solve/custom-call.0 | solution.py:28
  431.7 6.5 collective-permute-done.2
  439.0 36.5 %all-gather.30.cloned.1.call-done = f32[192,2048]{1,0:T(8,128)} async-done(((f32[192,128]{1,0:T(8,128)}), f32[192,2048]{1,0:T(8,128)}) %all-gather.30.cloned.1.call-update) | async-done | bytes 1572880 | tf_op jit(solution)/shard_map/all_gather | solution.py:45
  475.5 2.8 convolution_multiply_fusion.4
  479.8 38.5 %all-gather.48.cloned.1.call-done = f32[3072,192]{1,0:T(8,128)} async-done(((f32[192,192]{1,0:T(8,128)}), f32[3072,192]{1,0:T(8,128)}) %all-gather.48.cloned.1.call-update) | async-done | bytes 2359312 | tf_op jit(solution)/shard_map/all_gather | solution.py:48
  520.6 11.7 %cholesky.526 = f32[128,128]{1,0:T(8,128)S(1)} custom-call(f32[128,128]{1,0:T(8,128)S(1)} %cholesky.721), custom_call_target="Cholesky" | custom-call | tf_op jit(solution)/shard_map/jit(cholesky)/cholesky | solution.py:27
  533.0 9.8 custom-call.47
  543.2 5.8 cholesky.546
  551.2 19.7 %custom-call.48 = f32[2,128,128]{1,2,0:T(8,128)S(1)} custom-call(f32[2,128,128]{2,1,0:T(8,128)S(1)} %pad_maximum_fusion.3), custom_call_target="InvertDiagBlocksLowerTriangular" | custom-call | tf_op jit(solution)/shard_map/triangular_solve/custom-call.0 | solution.py:28
  572.9 6.5 collective-permute-done.3
  580.2 36.5 %all-gather.32.cloned.1.call-done = f32[192,2048]{1,0:T(8,128)} async-done(((f32[192,128]{1,0:T(8,128)}), f32[192,2048]{1,0:T(8,128)}) %all-gather.32.cloned.1.call-update) | async-done | bytes 1572880 | tf_op jit(solution)/shard_map/all_gather | solution.py:45
  616.7 2.8 convolution_multiply_fusion.3
  620.7 38.8 %all-gather.50.cloned.1.call-done = f32[3072,192]{1,0:T(8,128)} async-done(((f32[192,192]{1,0:T(8,128)}), f32[3072,192]{1,0:T(8,128)}) %all-gather.50.cloned.1.call-update) | async-done | bytes 2359312 | tf_op jit(solution)/shard_map/all_gather | solution.py:48
  661.8 11.7 %cholesky.564 = f32[128,128]{1,0:T(8,128)S(1)} custom-call(f32[128,128]{1,0:T(8,128)S(1)} %cholesky.724), custom_call_target="Cholesky" | custom-call | tf_op jit(solution)/shard_map/jit(cholesky)/cholesky | solution.py:27
  674.2 9.8 custom-call.49
  684.4 5.8 cholesky.584
  692.4 19.7 %custom-call.50 = f32[2,128,128]{1,2,0:T(8,128)S(1)} custom-call(f32[2,128,128]{2,1,0:T(8,128)S(1)} %pad_maximum_fusion.4), custom_call_target="InvertDiagBlocksLowerTriangular" | custom-call | tf_op jit(solution)/shard_map/triangular_solve/custom-call.0 | solution.py:28
  714.1 6.5 collective-permute-done.4
  721.3 36.5 %all-gather.34.cloned.1.call-done = f32[192,2048]{1,0:T(8,128)} async-done(((f32[192,128]{1,0:T(8,128)}), f32[192,2048]{1,0:T(8,128)}) %all-gather.34.cloned.1.call-update) | async-done | bytes 1572880 | tf_op jit(solution)/shard_map/all_gather | solution.py:45
  757.8 2.8 convolution_multiply_fusion.2
  762.1 38.5 %all-gather.52.cloned.1.call-done = f32[3072,192]{1,0:T(8,128)} async-done(((f32[192,192]{1,0:T(8,128)}), f32[3072,192]{1,0:T(8,128)}) %all-gather.52.cloned.1.call-update) | async-done | bytes 2359312 | tf_op jit(solution)/shard_map/all_gather | solution.py:48
  802.9 11.7 %cholesky.602 = f32[128,128]{1,0:T(8,128)S(1)} custom-call(f32[128,128]{1,0:T(8,128)S(1)} %cholesky.727), custom_call_target="Cholesky" | custom-call | tf_op jit(solution)/shard_map/jit(cholesky)/cholesky | solution.py:27
  815.4 9.8 custom-call.51
  825.6 5.8 cholesky.622
  833.5 19.7 %custom-call.52 = f32[2,128,128]{1,2,0:T(8,128)S(1)} custom-call(f32[2,128,128]{2,1,0:T(8,128)S(1)} %pad_maximum_fusion.5), custom_call_target="InvertDiagBlocksLowerTriangular" | custom-call | tf_op jit(solution)/shard_map/triangular_solve/custom-call.0 | solution.py:28
  855.2 6.5 collective-permute-done.5
  862.5 36.5 %all-gather.36.cloned.1.call-done = f32[192,2048]{1,0:T(8,128)} async-done(((f32[192,128]{1,0:T(8,128)}), f32[192,2048]{1,0:T(8,128)}) %all-gather.36.cloned.1.call-update) | async-done | bytes 1572880 | tf_op jit(solution)/shard_map/all_gather | solution.py:45
  899.0 2.8 convolution_multiply_fusion.1
  903.1 38.8 %all-gather.54.cloned.1.call-done = f32[3072,192]{1,0:T(8,128)} async-done(((f32[192,192]{1,0:T(8,128)}), f32[3072,192]{1,0:T(8,128)}) %all-gather.54.cloned.1.call-update) | async-done | bytes 2359312 | tf_op jit(solution)/shard_map/all_gather | solution.py:48
  944.1 11.7 %cholesky.640 = f32[128,128]{1,0:T(8,128)S(1)} custom-call(f32[128,128]{1,0:T(8,128)S(1)} %cholesky.730), custom_call_target="Cholesky" | custom-call | tf_op jit(solution)/shard_map/jit(cholesky)/cholesky | solution.py:27
  956.5 9.8 custom-call.53
  966.7 5.8 cholesky.660
  975.4 20.5 %custom-call.54 = f32[2,128,128]{1,2,0:T(8,128)S(1)} custom-call(f32[2,128,128]{2,1,0:T(8,128)} %pad_maximum_fusion.6), custom_call_target="InvertDiagBlocksLowerTriangular" | custom-call | tf_op jit(solution)/shard_map/triangular_solve/custom-call.0 | solution.py:28
  999.3 6.5 collective-permute-done.6
  1006.5 36.5 %all-gather.38.cloned.1.call-done = f32[192,2048]{1,0:T(8,128)} async-done(((f32[192,128]{1,0:T(8,128)}), f32[192,2048]{1,0:T(8,128)}) %all-gather.38.cloned.1.call-update) | async-done | bytes 1572880 | tf_op jit(solution)/shard_map/all_gather | solution.py:45
  1043.0 2.8 convolution_multiply_fusion
  1046.9 2.1 gather_fusion
  1065.2 20.7 %all-gather.56.cloned.1.call-done = f32[3072,192]{1,0:T(8,128)} async-done(((f32[192,192]{1,0:T(8,128)}), f32[3072,192]{1,0:T(8,128)}) %all-gather.56.cloned.1.call-update) | async-done | bytes 2359312 | tf_op jit(solution)/shard_map/all_gather | solution.py:48
  1088.2 11.7 %cholesky.678 = f32[128,128]{1,0:T(8,128)S(1)} custom-call(f32[128,128]{1,0:T(8,128)S(1)} %cholesky.733), custom_call_target="Cholesky" | custom-call | tf_op jit(solution)/shard_map/jit(cholesky)/cholesky | solution.py:27
  1100.6 9.8 custom-call.55
  1110.8 5.8 cholesky.698
  1120.8 19.9 %custom-call.56 = f32[2,128,128]{1,2,0:T(8,128)S(1)} custom-call(f32[2,128,128]{2,1,0:T(8,128)S(1)} %pad_maximum_fusion.7), custom_call_target="InvertDiagBlocksLowerTriangular" | custom-call | tf_op jit(solution)/shard_map/triangular_solve/custom-call.0 | solution.py:28
  (255 shorter events, 85.5 us)
Async XLA Ops:
  7.2 44.9 %copy-start = (f32[128,2048]{1,0:T(8,128)S(1)}, f32[128,2048]{1,0:T(8,128)}, u32[]{:S(2)}) copy-start(f32[128,2048]{1,0:T(8,128)} %param.7) | copy-start | bytes 3145732
  7.2 44.9 %all-gather.40.cloned.1.call-start = ((), (), s32[]{:S(2)}) async-start(), calls=%async_computation.7 | async-start | bytes 1671168 | tf_op jit(solution)/shard_map/all_gather | solution.py:45
  7.9 87.0 %all-gather.42.cloned.1.call-start = ((), (), s32[]{:S(2)}) async-start(), calls=%async_computation.8 | async-start | bytes 3342336 | tf_op jit(solution)/shard_map/all_gather | solution.py:48
  55.9 137.3 %all-gather.26.cloned.1.call-start = ((), (), s32[]{:S(2)}) async-start(), calls=%async_computation | async-start | bytes 1671168 | tf_op jit(solution)/shard_map/all_gather | solution.py:45
  148.2 7.8 collective-permute-start
  156.0 0.6 copy-start.3
  156.6 79.4 %all-gather.44.cloned.1.call-start = ((), (), s32[]{:S(2)}) async-start(), calls=%async_computation.9 | async-start | bytes 3342336 | tf_op jit(solution)/shard_map/all_gather | solution.py:48
  197.0 137.3 %all-gather.28.cloned.1.call-start = ((), (), s32[]{:S(2)}) async-start(), calls=%async_computation.1 | async-start | bytes 1671168 | tf_op jit(solution)/shard_map/all_gather | solution.py:45
  289.3 7.8 collective-permute-start.1
  297.1 0.6 copy-start.4
  297.8 79.4 %all-gather.46.cloned.1.call-start = ((), (), s32[]{:S(2)}) async-start(), calls=%async_computation.10 | async-start | bytes 3342336 | tf_op jit(solution)/shard_map/all_gather | solution.py:48
  338.2 137.3 %all-gather.30.cloned.1.call-start = ((), (), s32[]{:S(2)}) async-start(), calls=%async_computation.2 | async-start | bytes 1671168 | tf_op jit(solution)/shard_map/all_gather | solution.py:45
  430.5 7.8 collective-permute-start.2
  438.3 0.6 copy-start.5
  439.0 79.4 %all-gather.48.cloned.1.call-start = ((), (), s32[]{:S(2)}) async-start(), calls=%async_computation.11 | async-start | bytes 3342336 | tf_op jit(solution)/shard_map/all_gather | solution.py:48
  479.4 137.3 %all-gather.32.cloned.1.call-start = ((), (), s32[]{:S(2)}) async-start(), calls=%async_computation.3 | async-start | bytes 1671168 | tf_op jit(solution)/shard_map/all_gather | solution.py:45
  571.6 7.8 collective-permute-start.3
  579.5 0.6 copy-start.6
  580.1 79.4 %all-gather.50.cloned.1.call-start = ((), (), s32[]{:S(2)}) async-start(), calls=%async_computation.12 | async-start | bytes 3342336 | tf_op jit(solution)/shard_map/all_gather | solution.py:48
  620.5 137.3 %all-gather.34.cloned.1.call-start = ((), (), s32[]{:S(2)}) async-start(), calls=%async_computation.4 | async-start | bytes 1671168 | tf_op jit(solution)/shard_map/all_gather | solution.py:45
  712.8 7.8 collective-permute-start.4
  720.6 0.6 copy-start.7
  721.3 79.4 %all-gather.52.cloned.1.call-start = ((), (), s32[]{:S(2)}) async-start(), calls=%async_computation.13 | async-start | bytes 3342336 | tf_op jit(solution)/shard_map/all_gather | solution.py:48
  761.7 137.3 %all-gather.36.cloned.1.call-start = ((), (), s32[]{:S(2)}) async-start(), calls=%async_computation.5 | async-start | bytes 1671168 | tf_op jit(solution)/shard_map/all_gather | solution.py:45
  854.0 48.9 %copy-start.1 = (f32[64,128]{1,0:T(8,128)}, f32[64,128]{1,0:T(8,128)S(1)}, u32[]{:S(2)}) copy-start(f32[64,128]{1,0:T(8,128)S(1)} %fusion.74) | copy-start | bytes 98308
  854.0 7.8 collective-permute-start.5
  861.8 0.6 copy-start.8
  862.5 79.4 %all-gather.54.cloned.1.call-start = ((), (), s32[]{:S(2)}) async-start(), calls=%async_computation.14 | async-start | bytes 3342336 | tf_op jit(solution)/shard_map/all_gather | solution.py:48
  902.9 140.2 %all-gather.38.cloned.1.call-start = ((), (), s32[]{:S(2)}) async-start(), calls=%async_computation.6 | async-start | bytes 1671168 | tf_op jit(solution)/shard_map/all_gather | solution.py:45
  995.9 0.7 copy-start.10
  998.0 7.8 collective-permute-start.6
  1005.8 0.6 copy-start.9
  1006.5 79.4 %all-gather.56.cloned.1.call-start = ((), (), s32[]{:S(2)}) async-start(), calls=%async_computation.15 | async-start | bytes 3342336 | tf_op jit(solution)/shard_map/all_gather | solution.py:48
  1056.8 5.2 copy-start.2
Sparse Core Ops, SparseCore 0:
  9.8 42.2 all-gather.39
  56.0 38.8 all-gather.41
  156.8 36.3 all-gather.25
  197.2 38.8 all-gather.43
  297.9 36.3 all-gather.27
  338.3 38.8 all-gather.45
  439.1 36.3 all-gather.29
  479.5 38.8 all-gather.47
  580.2 36.3 all-gather.31
  620.6 38.8 all-gather.49
  721.4 36.3 all-gather.33
  761.8 38.8 all-gather.51
  862.6 36.3 all-gather.35
  903.0 38.8 all-gather.53
  1006.6 36.3 all-gather.37
  1047.0 38.8 all-gather.55
